TPU v7x, 512 devices: a whole 4x4x16 slice. The times are simulated.
512 devices in a mesh: wide: 128 (over z, x, core), narrow: 4 (over y).
Axes of the slice: x: 4, y: 4, z: 16, core: 2. Of those that a mesh axis runs over, the one named last changes fastest.
Arguments:
- tokens_in: bfloat16 [16384, 2560], P('wide', 'narrow'), may hold values from -6 to 6
- norm_gain: bfloat16 [2560], replicated, may hold values from 0.099609375 to 1.8984375
- query_weight: bfloat16 [2560, 2560], P('wide', 'narrow'), may hold values from -0.25 to 0.25
- key_weight: bfloat16 [2560, 640], P('wide', 'narrow'), may hold values from -0.125 to 0.125
- value_weight: bfloat16 [2560, 640], P('wide', 'narrow'), may hold values from -0.5 to 0.5
- out_weight: bfloat16 [2560, 2560], P('wide', 'narrow'), may hold values from -0.125 to 0.125
- cache_keys: bfloat16 [640, 131072], P('narrow', 'wide'), may hold values from -64 to 64
- cache_values: bfloat16 [640, 131072], P('narrow', 'wide'), may hold values from -24 to 24
- cached_len: int32 [32], replicated, may hold values from 1 to 4096, as said below
- append_slot: int32 [32], replicated, may hold values from 0 to 4095
- shard_owner: int32 [32], replicated, may hold values from 0 to 3
Outputs:
- attention_update: bfloat16 [16384, 2560], P('wide', 'narrow')
- appended_keys: bfloat16 [640, 131072], P('narrow', 'wide')
- appended_values: bfloat16 [640, 131072], P('narrow', 'wide')
Inputs may be any that keep to these rules, and one draw needn't show every extreme that they name: `cached_len`: each request's number of cached keys; some request holds 4096.
All inputs are finite; a program needn't handle non-finite values.
Results may differ from a plain program's by a relative error of at most 0.012.
The roundings to bfloat16 on the way count: a program that leaves them out, or rounds other values in their place, can miss the bound.
Values may be sent and summed in bfloat16 or wider, within the bound.
A program may use at most 64 MiB of HBM per device.

v0:
```python
import math
import numpy as np
import jax
import jax.numpy as jnp
from jax import lax
from jax.sharding import Mesh, PartitionSpec as P

HEAD_DIM = 80
WIN = 4096
GROUP_BITS = 2
GROUP = 4
EPSILON = 1e-05
ROPE_BASE = 10000.0
LOWEST = -1e30


def from_partner(block, axis, bit):
    count = lax.psum(1, axis)
    route = []
    for low in range(count):
        high = low | 1 << bit
        if high != low and high < count:
            route += [(low, high), (high, low)]
    return lax.ppermute(block, axis, route)


WIDE = ("z", "x", "c")


def gather_rows(block):
    rows = block.shape[0]
    plane = lax.all_gather(block, ("z", "x"), axis=0, tiled=False)
    both = lax.all_gather(plane, "c", axis=0, tiled=False)
    both = jnp.transpose(both, (1, 0, 2, 3))
    return both.reshape(-1, block.shape[1])


def rms_normed(rows_in, gain):
    values = rows_in.astype(jnp.float32)
    scaling = lax.rsqrt(jnp.mean(values * values, axis=-1, keepdims=True) + EPSILON)
    return (values * scaling * gain.astype(jnp.float32)).astype(jnp.bfloat16)


def rotate(values, positions):
    half_dim = values.shape[-1] // 2
    inverse = ROPE_BASE ** (-(jnp.arange(half_dim, dtype=jnp.float32) * (2.0 / values.shape[-1])))
    angles = positions.astype(jnp.float32)[:, None] * inverse[None, :]
    cos_part = jnp.cos(angles)[:, None, :]
    sin_part = jnp.sin(angles)[:, None, :]
    lower = values[..., :half_dim]
    higher = values[..., half_dim:]
    return jnp.concatenate(
        [lower * cos_part - higher * sin_part, higher * cos_part + lower * sin_part], axis=-1
    )


def ordered(mine, other, upper, along):
    first_half = jnp.where(upper, other, mine)
    second_half = jnp.where(upper, mine, other)
    return jnp.concatenate([first_half, second_half], axis=along)


def empty_state(row_count, groups, repeats):
    return (
        jnp.zeros((row_count, groups, repeats, HEAD_DIM), jnp.float32),
        jnp.full((row_count, groups, repeats), LOWEST, jnp.float32),
        jnp.zeros((row_count, groups, repeats), jnp.float32),
    )


def fold_keys(state, queries, query_pos, keys, values, key_pos, key_ok, widest):
    key_count = keys.shape[1]
    groups = queries.shape[1]
    block = math.gcd(key_count, widest)
    keys_split = keys.reshape(groups, HEAD_DIM, key_count)
    values_split = values.reshape(groups, HEAD_DIM, key_count)
    scale = HEAD_DIM ** (-0.5)

    def step(index, carry):
        accum, top_old, sum_old = carry
        start = index * block
        block_keys = lax.dynamic_slice_in_dim(keys_split, start, block, 2)
        block_values = lax.dynamic_slice_in_dim(values_split, start, block, 2)
        block_pos = lax.dynamic_slice_in_dim(key_pos, start, block, 0)
        block_ok = lax.dynamic_slice_in_dim(key_ok, start, block, 0)
        scores = (
            jnp.einsum("tgrd,gdk->tgrk", queries, block_keys, preferred_element_type=jnp.float32)
            * scale
        )
        allowed = (
            block_ok[None, :]
            & (block_pos[None, :] <= query_pos[:, None])
            & (query_pos[:, None] - block_pos[None, :] < WIN)
        )
        allowed = allowed[:, None, None, :]
        top_new = jnp.maximum(top_old, jnp.max(jnp.where(allowed, scores, LOWEST), axis=-1))
        weights = jnp.where(allowed, jnp.exp(scores - top_new[..., None]), 0.0)
        rescale = jnp.exp(top_old - top_new)
        sum_new = sum_old * rescale + jnp.sum(weights, axis=-1)
        mixed = jnp.einsum(
            "tgrk,gdk->tgrd",
            weights.astype(jnp.bfloat16),
            block_values,
            preferred_element_type=jnp.float32,
        )
        return (accum * rescale[..., None] + mixed, top_new, sum_new)

    return lax.fori_loop(0, key_count // block, step, state)


def shards(
    tokens_in,
    norm_gain,
    query_weight,
    key_weight,
    value_weight,
    out_weight,
    cache_keys,
    cache_values,
    cached_len,
    append_slot,
    shard_owner,
):
    whole = lax.all_gather(tokens_in, "narrow", axis=1, tiled=True)
    normed = rms_normed(whole, norm_gain)
    tok_rows = whole.shape[0]
    query_width = query_weight.shape[1]
    kv_width = key_weight.shape[1]
    local_heads = query_width // HEAD_DIM
    local_groups = kv_width // HEAD_DIM
    repeats = local_heads // local_groups
    columns = normed
    qkv = gather_rows(jnp.concatenate([query_weight, key_weight, value_weight], axis=1))
    qkv_sum = jnp.dot(columns, qkv, preferred_element_type=jnp.float32)
    query_sum = qkv_sum[:, :query_width]
    key_sum = qkv_sum[:, query_width : query_width + kv_width]
    value_sum = qkv_sum[:, query_width + kv_width :]
    position = lax.axis_index(WIDE)
    request = position // GROUP
    place = position % GROUP
    length = cached_len[request]
    offset = append_slot[request]
    owner = shard_owner[request]
    query_pos = length + place * tok_rows + jnp.arange(tok_rows, dtype=jnp.int32)
    queries = rotate(query_sum.reshape(tok_rows, local_heads, HEAD_DIM), query_pos).astype(
        jnp.bfloat16
    )
    queries = queries.reshape(tok_rows, local_groups, repeats, HEAD_DIM)
    new_keys = (
        rotate(key_sum.reshape(tok_rows, local_groups, HEAD_DIM), query_pos)
        .astype(jnp.bfloat16)
        .reshape(tok_rows, kv_width)
    )
    new_values = value_sum.astype(jnp.bfloat16)
    shard_rows = cache_keys.shape[1]
    within = jnp.arange(shard_rows, dtype=jnp.int32)
    cycle_mine = (place - owner) % GROUP * shard_rows + within
    old_keys, old_values = (cache_keys, cache_values)
    for bit in range(GROUP_BITS):
        upper = place // 2**bit % 2 == 1
        other_keys, other_values, other_old_keys, other_old_values = from_partner(
            (new_keys, new_values, old_keys, old_values), WIDE, bit
        )
        new_keys = ordered(new_keys, other_keys, upper, 0)
        new_values = ordered(new_values, other_values, upper, 0)
        old_keys = ordered(old_keys, other_old_keys, upper, 1)
        old_values = ordered(old_values, other_old_values, upper, 1)
    slot_index = jnp.arange(old_keys.shape[1], dtype=jnp.int32)
    cycle = (slot_index // shard_rows - owner) % GROUP * shard_rows + slot_index % shard_rows
    cached_pos = (cycle - offset + length) % WIN
    state = fold_keys(
        empty_state(tok_rows, local_groups, repeats),
        queries,
        query_pos,
        old_keys,
        old_values,
        cached_pos,
        cached_pos < length,
        512,
    )
    key_cols = new_keys.T
    value_cols = new_values.T
    new_count = key_cols.shape[1]
    new_pos = length + jnp.arange(new_count, dtype=jnp.int32)
    state = fold_keys(
        state,
        queries,
        query_pos,
        key_cols,
        value_cols,
        new_pos,
        jnp.ones((new_count,), dtype=bool),
        512,
    )
    accum, top_score, total = state
    attended = (accum / total[..., None]).astype(jnp.bfloat16).reshape(tok_rows, query_width)
    all_heads = lax.all_gather(attended, "narrow", axis=1, tiled=True)
    columns = all_heads
    update = jnp.dot(columns, gather_rows(out_weight), preferred_element_type=jnp.float32).astype(
        jnp.bfloat16
    )
    new_index = (cycle_mine - offset) % WIN
    written = new_index < new_count
    take_rows = jnp.minimum(new_index, new_count - 1)
    put_keys = jnp.where(written[None, :], jnp.take(key_cols, take_rows, axis=1), cache_keys)
    put_values = jnp.where(written[None, :], jnp.take(value_cols, take_rows, axis=1), cache_values)
    return (update, put_keys, put_values)


def solution(mesh):
    devices = mesh.devices
    wide_devices = devices[:, 0]
    xs = sorted({d.coords[0] for d in wide_devices})
    cores = sorted({getattr(d, "core_on_chip", 0) for d in wide_devices})
    n_x, n_c = (len(xs), len(cores))
    n_z = devices.shape[0] // (n_x * n_c)
    fine = Mesh(devices.reshape(n_z, n_x, n_c, devices.shape[1]), ("z", "x", "c", "narrow"))
    rows = P(WIDE, "narrow")
    cols = P("narrow", WIDE)
    in_specs = (rows, P(), rows, rows, rows, rows, cols, cols, P(), P(), P())
    out_specs = (rows, cols, cols)
    return jax.shard_map(shards, mesh=fine, in_specs=in_specs, out_specs=out_specs, check_vma=False)
```

profile of v0, /device:TPU:2, one launch (start us, length us, event | category | flops | bytes accessed | tf_op | source)
XLA Modules:
  0.0 497.3 jit_solution(6493536024206706948)
XLA Ops:
  7.2 0.7 all-gather.17.cloned.1.call-update
  7.9 1.5 maximum_bitcast_fusion
  9.5 145.7 %all-gather.17.cloned.1.call-done = bf16[64,20,640]{2,1,0:T(8,128)(2,1)} async-done(((bf16[1,20,640]{2,1,0:T(8,128)(2,1)}), bf16[64,20,640]{2,1,0:T(8,128)(2,1)}) %all-gather.17.cloned.1.call-update) | async-done | bytes 1638416 | tf_op jit(solution)/shard_map/all_gather | solution.py:32
  155.2 3.0 copy.36
  158.3 139.7 %all-gather.15.cloned.1.call-done = bf16[64,20,960]{2,1,0:T(8,128)(2,1)} async-done(((bf16[1,20,960]{2,1,0:T(8,128)(2,1)}), bf16[64,20,960]{2,1,0:T(8,128)(2,1)}) %all-gather.15.cloned.1.call-update) | async-done | bytes 2457616 | tf_op jit(solution)/shard_map/all_gather | solution.py:32
  298.0 4.8 copy.33
  302.9 0.9 copy-done.1
  303.8 1.9 collective-permute-start.2
  305.7 2.4 collective-permute-start
  308.2 1.0 copy.41
  310.3 1.0 copy.39
  313.9 0.7 compare_and_fusion
  314.6 1.9 broadcast_compare_fusion
  316.6 0.7 fusion.58
  317.3 1.9 add_select_fusion
  319.2 13.7 %all_gather.30 = bf16[128,2560]{1,0:T(8,128)(2,1)S(1)} all-gather(bf16[128,640]{1,0:T(8,128)(2,1)S(1)} %copy-done.3), channel_id=1, replica_groups=mesh['z'=16,'x'=4,'c'=2,'narrow'=4] {'narrow'}, dimensions={1}, use_global_device_ids=true | all-gather | bytes 819200 | tf_op jit(solution)/shard_map/all_gather | solution.py:124
  333.4 4.1 collective-permute-start.1
  337.7 2.1 collective-permute-start.3
  339.8 13.3 %collective-permute-done.1 = bf16[160,2048]{1,0:T(8,128)(2,1)S(1)} collective-permute-done((bf16[160,2048]{1,0:T(8,128)(2,1)S(1)}, bf16[160,2048]{1,0:T(8,128)(2,1)S(1)}, u32[]{:S(2)}, u32[]{:S(2)}) %collective-permute-start.1) | collective-permute-done | bytes 655392 | tf_op jit(solution)/shard_map/ppermute | solution.py:24
  353.4 1.2 pad_maximum_fusion
  354.6 10.1 %collective-permute-done.3 = bf16[160,2048]{1,0:T(8,128)(2,1)S(1)} collective-permute-done((bf16[160,2048]{1,0:T(8,128)(2,1)S(1)}, bf16[160,2048]{1,0:T(8,128)(2,1)S(1)}, u32[]{:S(2)}, u32[]{:S(2)}) %collective-permute-start.3) | collective-permute-done | bytes 655392 | tf_op jit(solution)/shard_map/ppermute | solution.py:24
  365.0 1.2 pad_maximum_fusion.1
  366.2 5.7 %copy.53 = bf16[2,64,20,640]{3,2,0,1:T(8,128)(2,1)} copy(bf16[2,64,20,640]{3,1,0,2:T(8,128)(2,1)} %bitcast.126) | data formatting | bytes 6553600 | tf_op jit(solution)/shard_map/all_gather | solution.py:33
  371.9 6.1 %reshape.253 = bf16[2560,640]{1,0:T(8,128)(2,1)} reshape(bf16[64,2,20,640]{3,2,1,0:T(8,128)(2,1)} %bitcast.123) | data formatting | bytes 6553600 | tf_op jit(solution)/shard_map/reshape | solution.py:35
  378.0 8.1 %copy.52 = bf16[2,64,20,960]{3,2,0,1:T(8,128)(2,1)} copy(bf16[2,64,20,960]{3,1,0,2:T(8,128)(2,1)} %bitcast.124) | data formatting | bytes 9830400 | tf_op jit(solution)/shard_map/all_gather | solution.py:33
  386.1 9.8 %reshape.246 = bf16[2560,960]{1,0:T(8,128)(2,1)} reshape(bf16[64,2,20,960]{3,2,1,0:T(8,128)(2,1)} %bitcast.122) | data formatting | bytes 9830400 | tf_op jit(solution)/shard_map/reshape | solution.py:35
  395.9 4.6 fusion.38
  400.6 1.9 collective-permute-start.6
  402.6 2.4 collective-permute-start.4
  405.1 39.9 %while.5 = (s32[]{:T(128)}, f32[128,2,4,80]{0,3,2,1:T(8,128)}, f32[128,2,4]{0,2,1:T(4,128)S(1)}, f32[128,2,4]{0,2,1:T(4,128)S(1)}, pred[4096]{0:T(1024)(128)(4,1...) while((s32[]{:T(128)}, f32[128,2,4,80]{0,3,2,1:T(8,128)}, ...), condition=%wide.region_4.5_spmd.clone, body=%wide.region_1.4_spmd.clone.sunk | while | flops 174118016 | bytes 10396435 | solution.py:108
  405.5 1.4 fusion.83
  407.9 1.5 fusion.86
  409.4 0.7 copy-done.9
  410.5 1.4 fusion.83
  412.9 1.5 fusion.86
  414.4 0.7 copy-done.9
  415.5 1.4 fusion.83
  417.9 1.5 fusion.86
  419.4 0.7 copy-done.9
  420.4 1.4 fusion.83
  422.9 1.5 fusion.86
  424.3 0.7 copy-done.9
  425.4 1.4 fusion.83
  427.8 1.5 fusion.86
  429.3 0.7 copy-done.9
  430.4 1.4 fusion.83
  432.8 1.5 fusion.86
  434.3 0.7 copy-done.9
  435.4 1.4 fusion.83
  437.8 1.5 fusion.86
  439.3 0.7 copy-done.9
  440.4 1.4 fusion.83
  442.8 1.5 fusion.86
  444.3 0.7 copy-done.9
  445.0 3.6 collective-permute-start.7
  448.7 2.4 collective-permute-start.5
  451.4 3.6 collective-permute-done.5
  456.7 14.5 %all_gather.35 = bf16[128,2560]{0,1:T(8,128)(2,1)} all-gather(bf16[128,640]{0,1:T(8,128)(2,1)S(1)} %bitcast.138), channel_id=1, replica_groups=mesh['z'=16,'x'=4,'c'=2,'narrow'=4] {'narrow'}, dimensions={1}, use_global_device_ids=true | all-gather | bytes 819200 | tf_op jit(solution)/shard_map/all_gather | solution.py:197
  471.4 5.0 %gather_fusion.1 = bf16[1024,160]{1,0:T(8,128)(2,1)} fusion(bf16[160,512]{0,1:T(8,128)(2,1)S(1)} %copy.40, s32[1024]{0:T(1024)S(1)} %fusion.58), kind=kCustom, calls=%fused_computation.1.clone | custom fusion | bytes 659456 | tf_op jit(solution)/shard_map/jit(_take)/gather | solution.py:206
  476.4 5.0 %gather_fusion = bf16[1024,160]{1,0:T(8,128)(2,1)} fusion(bf16[160,512]{0,1:T(8,128)(2,1)S(1)} %copy.38, s32[1024]{0:T(1024)S(1)} %fusion.58), kind=kCustom, calls=%fused_computation.clone | custom fusion | bytes 659456 | tf_op jit(solution)/shard_map/jit(_take)/gather | solution.py:205
  481.4 3.0 bitcast_select_fusion.2
  484.4 1.9 copy.42
  486.3 1.9 copy.43
  488.3 2.5 convolution_convert_fusion
  (160 shorter events, 16.9 us)
Async XLA Ops:
  7.2 148.1 %all-gather.17.cloned.1.call-start = ((), (), s32[]{:S(2)}) async-start(), calls=%async_computation.3 | async-start | bytes 1996800 | tf_op jit(solution)/shard_map/all_gather | solution.py:32
  7.9 290.1 %all-gather.15.cloned.1.call-start = ((), (), s32[]{:S(2)}) async-start(), calls=%async_computation.2 | async-start | bytes 3194880 | tf_op jit(solution)/shard_map/all_gather | solution.py:32
  9.5 356.8 %all-gather.13.cloned.1.call-start = ((), (), s32[]{:S(2)}) async-start(), calls=%async_computation.1 | async-start | bytes 4915200 | tf_op jit(solution)/shard_map/all_gather | solution.py:33
  158.2 219.8 %all-gather.11.cloned.1.call-start = ((), (), s32[]{:S(2)}) async-start(), calls=%async_computation | async-start | bytes 7864320 | tf_op jit(solution)/shard_map/all_gather | solution.py:33
  302.8 1.0 copy-start.1
  302.8 2.9 copy-start.2
  302.8 6.4 %copy-start.5 = (s32[32]{0:T(128)S(1)}, s32[32]{0:T(128)}, u32[]{:S(2)}) copy-start(s32[32]{0:T(128)} %param.25) | copy-start | bytes 388
  302.8 8.5 %copy-start.4 = (bf16[2560]{0:T(1024)(128)(2,1)S(1)}, bf16[2560]{0:T(1024)(128)(2,1)}, u32[]{:S(2)}) copy-start(bf16[2560]{0:T(1024)(128)(2,1)} %param.16) | copy-start | bytes 15364
  302.8 8.5 %copy-start.6 = (s32[32]{0:T(128)S(1)}, s32[32]{0:T(128)}, u32[]{:S(2)}) copy-start(s32[32]{0:T(128)} %param.23) | copy-start | bytes 388
  302.8 9.1 %copy-start.7 = (s32[32]{0:T(128)S(1)}, s32[32]{0:T(128)}, u32[]{:S(2)}) copy-start(s32[32]{0:T(128)} %param.24) | copy-start | bytes 388
  302.8 16.4 %copy-start.3 = (bf16[128,640]{1,0:T(8,128)(2,1)S(1)}, bf16[128,640]{1,0:T(8,128)(2,1)}, u32[]{:S(2)}) copy-start(bf16[128,640]{1,0:T(8,128)(2,1)} %param.15) | copy-start | bytes 491524
  303.8 29.5 %collective-permute-start.2 = (bf16[160,1024]{1,0:T(8,128)(2,1)S(1)}, bf16[160,1024]{1,0:T(8,128)(2,1)S(1)}, u32[]{:S(2)}, u32[]{:S(2)}) collective-permute-start(bf16[160,1024]{1,0:T(8,128)(2,1)S(1)} %copy-done.1), channel_id=1, source_target_pairs={{0,4},{4,0},{8,12},{12,8},{16,20},{20,16},{24,28},{28,24},{32,36},... | collective-permute-start | bytes 983048 | tf_op jit(solution)/shard_map/ppermute | solution.py:24
  305.7 27.6 %collective-permute-start = (bf16[160,1024]{1,0:T(8,128)(2,1)S(1)}, bf16[160,1024]{1,0:T(8,128)(2,1)S(1)}, u32[]{:S(2)}, u32[]{:S(2)}) collective-permute-start(bf16[160,1024]{1,0:T(8,128)(2,1)S(1)} %copy-done.2), channel_id=1, source_target_pairs={{0,4},{4,0},{8,12},{12,8},{16,20},{20,16},{24,28},{28,24},{32,36},... | collective-permute-start | bytes 983048 | tf_op jit(solution)/shard_map/ppermute | solution.py:24
  333.4 19.7 %collective-permute-start.1 = (bf16[160,2048]{1,0:T(8,128)(2,1)S(1)}, bf16[160,2048]{1,0:T(8,128)(2,1)S(1)}, u32[]{:S(2)}, u32[]{:S(2)}) collective-permute-start(bf16[160,2048]{1,0:T(8,128)(2,1)S(1)} %pad_maximum_fusion.2), channel_id=1, source_target_pairs={{0,8},{8,0},{4,12},{12,4},{16,24},{24,16},{20,28},{28,20},{32,40},... | collective-permute-start | bytes 1966088 | tf_op jit(solution)/shard_map/ppermute | solution.py:24
  337.7 27.1 %collective-permute-start.3 = (bf16[160,2048]{1,0:T(8,128)(2,1)S(1)}, bf16[160,2048]{1,0:T(8,128)(2,1)S(1)}, u32[]{:S(2)}, u32[]{:S(2)}) collective-permute-start(bf16[160,2048]{1,0:T(8,128)(2,1)S(1)} %pad_maximum_fusion.3), channel_id=1, source_target_pairs={{0,8},{8,0},{4,12},{12,4},{16,24},{24,16},{20,28},{28,20},{32,40},... | collective-permute-start | bytes 1966088 | tf_op jit(solution)/shard_map/ppermute | solution.py:24
  400.6 44.3 %collective-permute-start.6 = (bf16[128,160]{0,1:T(8,128)(2,1)S(1)}, bf16[128,160]{0,1:T(8,128)(2,1)S(1)}, u32[]{:S(2)}, u32[]{:S(2)}) collective-permute-start(bf16[128,160]{0,1:T(8,128)(2,1)S(1)} %slice.49), channel_id=1, source_target_pairs={{0,4},{4,0},{8,12},{12,8},{16,20},{20,16},{24,28},{28,24},{32,36},... | collective-permute-start | bytes 122888 | tf_op jit(solution)/shard_map/ppermute | solution.py:24
  402.6 42.4 %collective-permute-start.4 = (bf16[128,160]{0,1:T(8,128)(2,1)S(1)}, bf16[128,160]{0,1:T(8,128)(2,1)S(1)}, u32[]{:S(2)}, u32[]{:S(2)}) collective-permute-start(bf16[128,160]{0,1:T(8,128)(2,1)S(1)} %bitcast.136), channel_id=1, source_target_pairs={{0,4},{4,0},{8,12},{12,8},{16,20},{20,16},{24,28},{28,24},{32,36},... | collective-permute-start | bytes 122888 | tf_op jit(solution)/shard_map/ppermute | solution.py:24
  406.9 1.0 copy-start.8
  409.4 0.7 copy-start.9
  411.9 1.0 copy-start.8
  414.4 0.7 copy-start.9
  416.9 1.0 copy-start.8
  419.3 0.7 copy-start.9
  421.9 1.0 copy-start.8
  424.3 0.7 copy-start.9
  426.9 1.0 copy-start.8
  429.3 0.7 copy-start.9
  431.8 1.0 copy-start.8
  434.3 0.7 copy-start.9
  436.8 1.0 copy-start.8
  439.3 0.7 copy-start.9
  441.8 1.0 copy-start.8
  444.2 0.7 copy-start.9
  445.0 6.3 %collective-permute-start.7 = (bf16[256,160]{0,1:T(8,128)(2,1)S(1)}, bf16[256,160]{0,1:T(8,128)(2,1)S(1)}, u32[]{:S(2)}, u32[]{:S(2)}) collective-permute-start(bf16[256,160]{0,1:T(8,128)(2,1)S(1)} %pad_maximum_fusion.8), channel_id=1, source_target_pairs={{0,8},{8,0},{4,12},{12,4},{16,24},{24,16},{20,28},{28,20},{32,40},... | collective-permute-start | bytes 245768 | tf_op jit(solution)/shard_map/ppermute | solution.py:24
  448.7 6.3 %collective-permute-start.5 = (bf16[256,160]{0,1:T(8,128)(2,1)S(1)}, bf16[256,160]{0,1:T(8,128)(2,1)S(1)}, u32[]{:S(2)}, u32[]{:S(2)}) collective-permute-start(bf16[256,160]{0,1:T(8,128)(2,1)S(1)} %pad_maximum_fusion.7), channel_id=1, source_target_pairs={{0,8},{8,0},{4,12},{12,4},{16,24},{24,16},{20,28},{28,20},{32,40},... | collective-permute-start | bytes 245768 | tf_op jit(solution)/shard_map/ppermute | solution.py:24
  455.1 1.0 copy-start.10
  481.4 6.9 %copy-start = (bf16[2560,640]{1,0:T(8,128)(2,1)S(1)}, bf16[2560,640]{1,0:T(8,128)(2,1)}, u32[]{:S(2)}) copy-start(bf16[2560,640]{1,0:T(8,128)(2,1)} %reshape.253) | copy-start | bytes 9830404
Sparse Core Ops, SparseCore 0:
  11.0 144.2 all-gather.16
  158.7 139.1 all-gather.14
  300.1 18.8 all-gather.12
  320.9 27.0 all-gather.10
where the time goes:
time: 499 us; the launch traced here: 497 us
  waiting for transfers between devices  313 us (63%)
  local copies, waits for them, and re-layouts  67.2 us (13%)
  matrix products  31.3 us (6%)
  blocking collectives  28.1 us (6%)
  starting transfers between devices  21 us (4%)
  other arithmetic  20.2 us (4%)
  between operations  15.5 us (3%)
    all_gather x2, waiting for transfers between devices, gather_rows(): plane = lax.all_gather(block, ('z', 'x'), axis=0, tiled=False)  285 us
    ppermute x8, waiting for transfers between devices, from_partner(): return lax.ppermute(block, axis, route)  27.3 us
    ppermute x8, starting transfers between devices, from_partner(): return lax.ppermute(block, axis, route)  20.9 us
    reshape x2, local copies, waits for them, and re-layouts, gather_rows(): return both.reshape(-1, block.shape[1])  15.9 us
    all_gather x1, blocking collectives, shards(): all_heads = lax.all_gather(attended, 'narrow', axis=1, tiled=True)  14.5 us
    all_gather x2, local copies, waits for them, and re-layouts, gather_rows(): both = lax.all_gather(plane, 'c', axis=0, tiled=False)  13.8 us
    all_gather x1, blocking collectives, shards(): whole = lax.all_gather(tokens_in, 'narrow', axis=1, tiled=True)  13.7 us
    dot_general x9, matrix products, step(): jnp.einsum('tgrk,gdk->tgrd', weights.astype(jnp.bfloat16), block_values,...  12.2 us
  transfers between devices with their start and end apart: 12, of which 6 were waited for; matrix products, arithmetic and copies ran while one was open for 13% of the time, Pallas kernels for 0%

commit v1 on v0

--- a/solution.py
+++ b/solution.py
@@ -12,6 +12,11 @@
 EPSILON = 1e-05
 ROPE_BASE = 10000.0
 LOWEST = -1e30
+
+
+def tiled_gather(x, axis, dim):
+    copies = jnp.concatenate([x] * lax.axis_size(axis), axis=dim)
+    return lax.all_to_all(copies, axis, dim, dim, tiled=True)
 
 
 def from_partner(block, axis, bit):
@@ -194,7 +199,7 @@
     )
     accum, top_score, total = state
     attended = (accum / total[..., None]).astype(jnp.bfloat16).reshape(tok_rows, query_width)
-    all_heads = lax.all_gather(attended, "narrow", axis=1, tiled=True)
+    all_heads = tiled_gather(attended, "narrow", 1)
     columns = all_heads
     update = jnp.dot(columns, gather_rows(out_weight), preferred_element_type=jnp.float32).astype(
         jnp.bfloat16

time: 499 us -> 450 us (0.902)
  the two profiles are of different devices: /device:TPU:2 before, /device:TPU:10 now
where the time goes in v1:
time: 450 us; the launch traced here: 448 us
  waiting for transfers between devices  268 us (60%)
  local copies, waits for them, and re-layouts  70.5 us (16%)
  matrix products  31.6 us (7%)
  starting transfers between devices  26.8 us (6%)
  other arithmetic  20.2 us (4%)
  between operations  15.6 us (3%)
  blocking collectives  14.3 us (3%)
    all_gather x2, waiting for transfers between devices, gather_rows(): plane = lax.all_gather(block, ('z', 'x'), axis=0, tiled=False)  222 us
    ppermute x8, waiting for transfers between devices, from_partner(): return lax.ppermute(block, axis, route)  24.2 us
    all_gather x2, waiting for transfers between devices, gather_rows(): both = lax.all_gather(plane, 'c', axis=0, tiled=False)  21.7 us
    ppermute x8, starting transfers between devices, from_partner(): return lax.ppermute(block, axis, route)  20.6 us
    reshape x2, local copies, waits for them, and re-layouts, gather_rows(): return both.reshape(-1, block.shape[1])  15.9 us
    all_gather x1, blocking collectives, shards(): whole = lax.all_gather(tokens_in, 'narrow', axis=1, tiled=True)  14.3 us
    all_gather x2, local copies, waits for them, and re-layouts, gather_rows(): both = lax.all_gather(plane, 'c', axis=0, tiled=False)  13.9 us
    dot_general x9, matrix products, step(): jnp.einsum('tgrk,gdk->tgrd', weights.astype(jnp.bfloat16), block_values,...  12.2 us
  transfers between devices with their start and end apart: 13, of which 7 were waited for; matrix products, arithmetic and copies ran while one was open for 24% of the time, Pallas kernels for 0%

profile of v1, /device:TPU:10, one launch (start us, length us, event | category | flops | bytes accessed | tf_op | source)
XLA Modules:
  0.0 447.6 jit_solution(8138348600503686866)
XLA Ops:
  7.2 1.5 maximum_bitcast_fusion
  9.5 148.7 %all-gather.15.cloned.1.call-done = bf16[64,20,960]{2,1,0:T(8,128)(2,1)} async-done(((bf16[1,20,960]{2,1,0:T(8,128)(2,1)}), bf16[64,20,960]{2,1,0:T(8,128)(2,1)}) %all-gather.15.cloned.1.call-update) | async-done | bytes 2457616 | tf_op jit(solution)/shard_map/all_gather | solution.py:37
  158.3 4.8 %copy.48 = bf16[64,20,960]{2,0,1:T(8,128)(2,1)} copy(bf16[64,20,960]{2,1,0:T(8,128)(2,1)} %all-gather.15.cloned.1.call-done) | data formatting | bytes 4915200 | tf_op jit(solution)/shard_map/all_gather | solution.py:37
  163.2 0.9 copy-done.1
  164.1 1.9 collective-permute-start.2
  166.0 2.4 collective-permute-start
  168.5 1.0 copy.58
  170.9 1.0 copy.56
  174.4 2.0 broadcast_compare_fusion
  176.4 2.0 add_select_fusion
  178.4 14.3 %all_gather.27 = bf16[128,2560]{1,0:T(8,128)(2,1)S(1)} all-gather(bf16[128,640]{1,0:T(8,128)(2,1)S(1)} %copy-done.3), channel_id=1, replica_groups=mesh['z'=16,'x'=4,'c'=2,'narrow'=4] {'narrow'}, dimensions={1}, use_global_device_ids=true | all-gather | bytes 819200 | tf_op jit(solution)/shard_map/all_gather | solution.py:129
  193.3 4.1 collective-permute-start.1
  197.5 1.9 collective-permute-start.3
  199.5 13.5 %collective-permute-done.1 = bf16[160,2048]{1,0:T(8,128)(2,1)S(1)} collective-permute-done((bf16[160,2048]{1,0:T(8,128)(2,1)S(1)}, bf16[160,2048]{1,0:T(8,128)(2,1)S(1)}, u32[]{:S(2)}, u32[]{:S(2)}) %collective-permute-start.1) | collective-permute-done | bytes 655392 | tf_op jit(solution)/shard_map/ppermute | solution.py:29
  213.3 1.2 pad_maximum_fusion
  214.5 8.4 %collective-permute-done.3 = bf16[160,2048]{1,0:T(8,128)(2,1)S(1)} collective-permute-done((bf16[160,2048]{1,0:T(8,128)(2,1)S(1)}, bf16[160,2048]{1,0:T(8,128)(2,1)S(1)}, u32[]{:S(2)}, u32[]{:S(2)}) %collective-permute-start.3) | collective-permute-done | bytes 655392 | tf_op jit(solution)/shard_map/ppermute | solution.py:29
  223.2 1.2 pad_maximum_fusion.1
  224.3 72.8 %all-gather.17.cloned.1.call-done = bf16[64,20,640]{2,1,0:T(8,128)(2,1)} async-done(((bf16[1,20,640]{2,1,0:T(8,128)(2,1)}), bf16[64,20,640]{2,1,0:T(8,128)(2,1)}) %all-gather.17.cloned.1.call-update) | async-done | bytes 1638416 | tf_op jit(solution)/shard_map/all_gather | solution.py:37
  297.1 3.0 copy.53
  300.1 21.6 %all-gather.11.cloned.1.call-done = bf16[128,20,960]{2,0,1:T(8,128)(2,1)} async-done(((bf16[64,20,960]{2,0,1:T(8,128)(2,1)}), bf16[128,20,960]{2,0,1:T(8,128)(2,1)}) %all-gather.11.cloned.1.call-update) | async-done | bytes 4915216 | tf_op jit(solution)/shard_map/all_gather | solution.py:38
  321.7 8.1 %copy.69 = bf16[2,64,20,960]{3,2,0,1:T(8,128)(2,1)} copy(bf16[2,64,20,960]{3,1,0,2:T(8,128)(2,1)} %bitcast.125) | data formatting | bytes 9830400 | tf_op jit(solution)/shard_map/all_gather | solution.py:38
  329.9 9.8 %reshape.256 = bf16[2560,960]{1,0:T(8,128)(2,1)} reshape(bf16[64,2,20,960]{3,2,1,0:T(8,128)(2,1)} %bitcast.123) | data formatting | bytes 9830400 | tf_op jit(solution)/shard_map/reshape | solution.py:40
  339.6 5.0 %fusion.38 = f32[128,960]{0,1:T(8,128)S(1)} fusion(bf16[2560,960]{1,0:T(8,128)(2,1)} %reshape.256, bf16[128,2560]{1,0:T(8,128)(2,1)S(1)} %all_gather.27, f32[2560]{0:T(1024)S(1)} %convert_element_type.43, f32[128]{0:T(128)S(1)} %add_rsqrt_fusion), kind=kOutput, calls=%fused_computation.56 | convolution fusion | flops 630456320 | bytes 6072832 | tf_op jit(solution)/shard_map/dot_general | solution.py:139
  344.7 2.3 collective-permute-start.6
  347.0 2.3 collective-permute-start.4
  349.3 39.9 %while.5 = (s32[]{:T(128)}, f32[128,2,4,80]{0,3,2,1:T(8,128)}, f32[128,2,4]{0,2,1:T(4,128)S(1)}, f32[128,2,4]{0,2,1:T(4,128)S(1)}, pred[4096]{0:T(1024)(128)(4,1...) while((s32[]{:T(128)}, f32[128,2,4,80]{0,3,2,1:T(8,128)}, ...), condition=%wide.region_4.5_spmd.clone, body=%wide.region_1.4_spmd.clone.sunk | while | flops 174118016 | bytes 10396435 | solution.py:113
  349.7 1.4 fusion.83
  352.1 1.5 fusion.86
  353.6 0.7 copy-done.9
  354.7 1.4 fusion.83
  357.1 1.5 fusion.86
  358.6 0.7 copy-done.9
  359.7 1.4 fusion.83
  362.1 1.5 fusion.86
  363.6 0.7 copy-done.9
  364.6 1.4 fusion.83
  367.1 1.5 fusion.86
  368.6 0.7 copy-done.9
  369.6 1.4 fusion.83
  372.0 1.5 fusion.86
  373.5 0.7 copy-done.9
  374.6 1.4 fusion.83
  377.0 1.5 fusion.86
  378.5 0.7 copy-done.9
  379.6 1.4 fusion.83
  382.0 1.5 fusion.86
  383.5 0.7 copy-done.9
  384.6 1.4 fusion.83
  387.0 1.5 fusion.86
  389.2 2.5 collective-permute-start.5
  391.7 3.4 collective-permute-start.7
  395.1 0.7 collective-permute-done.5
  396.4 1.6 collective-permute-done.7
  399.3 0.9 concatenate.60
  400.2 5.9 %all-to-all-start = ((bf16[128,4,640]{2,0,1:T(8,128)(2,1)}), bf16[128,4,640]{2,0,1:T(8,128)(2,1)}, u32[]{:S(2)}, u32[]{:S(2)}) async-start(bf16[128,4,640]{2,0,1:T(8,128)(2,1)} %concatenate.60), calls=%async_computation | async-start | bytes 1310720 | tf_op jit(solution)/shard_map/all_to_all | solution.py:19
  407.5 5.7 %copy.70 = bf16[2,64,20,640]{3,2,0,1:T(8,128)(2,1)} copy(bf16[2,64,20,640]{3,1,0,2:T(8,128)(2,1)} %bitcast.127) | data formatting | bytes 6553600 | tf_op jit(solution)/shard_map/all_gather | solution.py:38
  413.2 6.1 %reshape.262 = bf16[2560,640]{1,0:T(8,128)(2,1)} reshape(bf16[64,2,20,640]{3,2,1,0:T(8,128)(2,1)} %bitcast.124) | data formatting | bytes 6553600 | tf_op jit(solution)/shard_map/reshape | solution.py:40
  419.6 5.0 %gather_fusion.1 = bf16[1024,160]{1,0:T(8,128)(2,1)} fusion(bf16[160,512]{0,1:T(8,128)(2,1)S(1)} %copy.57, s32[1024]{0:T(1024)S(1)} %fusion.58), kind=kCustom, calls=%fused_computation.1.clone | custom fusion | bytes 659456 | tf_op jit(solution)/shard_map/jit(_take)/gather | solution.py:211
  424.6 5.0 %gather_fusion = bf16[1024,160]{1,0:T(8,128)(2,1)} fusion(bf16[160,512]{0,1:T(8,128)(2,1)S(1)} %copy.55, s32[1024]{0:T(1024)S(1)} %fusion.58), kind=kCustom, calls=%fused_computation.clone | custom fusion | bytes 659456 | tf_op jit(solution)/shard_map/jit(_take)/gather | solution.py:210
  429.6 2.9 bitcast_select_fusion.2
  432.5 1.9 copy.59
  434.5 1.9 copy.60
  436.4 2.2 copy.52
  438.6 2.5 convolution_convert_fusion
  (164 shorter events, 19.6 us)
Async XLA Ops:
  7.2 151.1 %all-gather.15.cloned.1.call-start = ((), (), s32[]{:S(2)}) async-start(), calls=%async_computation.3 | async-start | bytes 3194880 | tf_op jit(solution)/shard_map/all_gather | solution.py:37
  8.7 288.4 %all-gather.17.cloned.1.call-start = ((), (), s32[]{:S(2)}) async-start(), calls=%async_computation.4 | async-start | bytes 1996800 | tf_op jit(solution)/shard_map/all_gather | solution.py:37
  9.5 312.3 %all-gather.11.cloned.1.call-start = ((), (), s32[]{:S(2)}) async-start(), calls=%async_computation.1 | async-start | bytes 7864320 | tf_op jit(solution)/shard_map/all_gather | solution.py:38
  163.1 1.0 copy-start.1
  163.1 2.9 copy-start.2
  163.1 6.4 %copy-start.5 = (s32[32]{0:T(128)S(1)}, s32[32]{0:T(128)}, u32[]{:S(2)}) copy-start(s32[32]{0:T(128)} %param.25) | copy-start | bytes 388
  163.1 8.8 %copy-start.4 = (bf16[2560]{0:T(1024)(128)(2,1)S(1)}, bf16[2560]{0:T(1024)(128)(2,1)}, u32[]{:S(2)}) copy-start(bf16[2560]{0:T(1024)(128)(2,1)} %param.16) | copy-start | bytes 15364
  163.1 8.8 %copy-start.6 = (s32[32]{0:T(128)S(1)}, s32[32]{0:T(128)}, u32[]{:S(2)}) copy-start(s32[32]{0:T(128)} %param.23) | copy-start | bytes 388
  163.1 9.4 %copy-start.7 = (s32[32]{0:T(128)S(1)}, s32[32]{0:T(128)}, u32[]{:S(2)}) copy-start(s32[32]{0:T(128)} %param.24) | copy-start | bytes 388
  163.1 15.3 %copy-start.3 = (bf16[128,640]{1,0:T(8,128)(2,1)S(1)}, bf16[128,640]{1,0:T(8,128)(2,1)}, u32[]{:S(2)}) copy-start(bf16[128,640]{1,0:T(8,128)(2,1)} %param.15) | copy-start | bytes 491524
  163.1 244.4 %all-gather.13.cloned.1.call-start = ((), (), s32[]{:S(2)}) async-start(), calls=%async_computation.2 | async-start | bytes 4915200 | tf_op jit(solution)/shard_map/all_gather | solution.py:38
  164.1 29.0 %collective-permute-start.2 = (bf16[160,1024]{1,0:T(8,128)(2,1)S(1)}, bf16[160,1024]{1,0:T(8,128)(2,1)S(1)}, u32[]{:S(2)}, u32[]{:S(2)}) collective-permute-start(bf16[160,1024]{1,0:T(8,128)(2,1)S(1)} %copy-done.1), channel_id=1, source_target_pairs={{0,4},{4,0},{8,12},{12,8},{16,20},{20,16},{24,28},{28,24},{32,36},... | collective-permute-start | bytes 983048 | tf_op jit(solution)/shard_map/ppermute | solution.py:29
  166.0 27.1 %collective-permute-start = (bf16[160,1024]{1,0:T(8,128)(2,1)S(1)}, bf16[160,1024]{1,0:T(8,128)(2,1)S(1)}, u32[]{:S(2)}, u32[]{:S(2)}) collective-permute-start(bf16[160,1024]{1,0:T(8,128)(2,1)S(1)} %copy-done.2), channel_id=1, source_target_pairs={{0,4},{4,0},{8,12},{12,8},{16,20},{20,16},{24,28},{28,24},{32,36},... | collective-permute-start | bytes 983048 | tf_op jit(solution)/shard_map/ppermute | solution.py:29
  193.3 19.7 %collective-permute-start.1 = (bf16[160,2048]{1,0:T(8,128)(2,1)S(1)}, bf16[160,2048]{1,0:T(8,128)(2,1)S(1)}, u32[]{:S(2)}, u32[]{:S(2)}) collective-permute-start(bf16[160,2048]{1,0:T(8,128)(2,1)S(1)} %pad_maximum_fusion.2), channel_id=1, source_target_pairs={{0,8},{8,0},{4,12},{12,4},{16,24},{24,16},{20,28},{28,20},{32,40},... | collective-permute-start | bytes 1966088 | tf_op jit(solution)/shard_map/ppermute | solution.py:29
  197.5 25.3 %collective-permute-start.3 = (bf16[160,2048]{1,0:T(8,128)(2,1)S(1)}, bf16[160,2048]{1,0:T(8,128)(2,1)S(1)}, u32[]{:S(2)}, u32[]{:S(2)}) collective-permute-start(bf16[160,2048]{1,0:T(8,128)(2,1)S(1)} %pad_maximum_fusion.3), channel_id=1, source_target_pairs={{0,8},{8,0},{4,12},{12,4},{16,24},{24,16},{20,28},{28,20},{32,40},... | collective-permute-start | bytes 1966088 | tf_op jit(solution)/shard_map/ppermute | solution.py:29
  344.7 44.5 %collective-permute-start.6 = (bf16[128,160]{0,1:T(8,128)(2,1)S(1)}, bf16[128,160]{0,1:T(8,128)(2,1)S(1)}, u32[]{:S(2)}, u32[]{:S(2)}) collective-permute-start(bf16[128,160]{0,1:T(8,128)(2,1)S(1)} %slice.49), channel_id=1, source_target_pairs={{0,4},{4,0},{8,12},{12,8},{16,20},{20,16},{24,28},{28,24},{32,36},... | collective-permute-start | bytes 122888 | tf_op jit(solution)/shard_map/ppermute | solution.py:29
  347.0 42.2 %collective-permute-start.4 = (bf16[128,160]{0,1:T(8,128)(2,1)S(1)}, bf16[128,160]{0,1:T(8,128)(2,1)S(1)}, u32[]{:S(2)}, u32[]{:S(2)}) collective-permute-start(bf16[128,160]{0,1:T(8,128)(2,1)S(1)} %bitcast.138), channel_id=1, source_target_pairs={{0,4},{4,0},{8,12},{12,8},{16,20},{20,16},{24,28},{28,24},{32,36},... | collective-permute-start | bytes 122888 | tf_op jit(solution)/shard_map/ppermute | solution.py:29
  351.1 1.0 copy-start.8
  353.6 0.7 copy-start.9
  356.1 1.0 copy-start.8
  358.6 0.7 copy-start.9
  361.1 1.0 copy-start.8
  363.5 0.7 copy-start.9
  366.1 1.0 copy-start.8
  368.5 0.7 copy-start.9
  371.1 1.0 copy-start.8
  373.5 0.7 copy-start.9
  376.1 1.0 copy-start.8
  378.5 0.7 copy-start.9
  381.0 1.0 copy-start.8
  383.5 0.7 copy-start.9
  386.0 1.0 copy-start.8
  388.5 0.7 copy-start.9
  389.2 6.6 %collective-permute-start.5 = (bf16[256,160]{0,1:T(8,128)(2,1)S(1)}, bf16[256,160]{0,1:T(8,128)(2,1)S(1)}, u32[]{:S(2)}, u32[]{:S(2)}) collective-permute-start(bf16[256,160]{0,1:T(8,128)(2,1)S(1)} %pad_maximum_fusion.7), channel_id=1, source_target_pairs={{0,8},{8,0},{4,12},{12,4},{16,24},{24,16},{20,28},{28,20},{32,40},... | collective-permute-start | bytes 245768 | tf_op jit(solution)/shard_map/ppermute | solution.py:29
  391.7 6.3 %collective-permute-start.7 = (bf16[256,160]{0,1:T(8,128)(2,1)S(1)}, bf16[256,160]{0,1:T(8,128)(2,1)S(1)}, u32[]{:S(2)}, u32[]{:S(2)}) collective-permute-start(bf16[256,160]{0,1:T(8,128)(2,1)S(1)} %pad_maximum_fusion.8), channel_id=1, source_target_pairs={{0,8},{8,0},{4,12},{12,4},{16,24},{24,16},{20,28},{28,20},{32,40},... | collective-permute-start | bytes 245768 | tf_op jit(solution)/shard_map/ppermute | solution.py:29
  396.4 2.2 copy-start.10
  400.2 36.2 %all-to-all-start = ((bf16[128,4,640]{2,0,1:T(8,128)(2,1)}), bf16[128,4,640]{2,0,1:T(8,128)(2,1)}, u32[]{:S(2)}, u32[]{:S(2)}) async-start(bf16[128,4,640]{2,0,1:T(8,128)(2,1)} %concatenate.60), calls=%async_computation | async-start | bytes 1310720 | tf_op jit(solution)/shard_map/all_to_all | solution.py:19
  429.6 9.0 %copy-start = (bf16[2560,640]{1,0:T(8,128)(2,1)S(1)}, bf16[2560,640]{1,0:T(8,128)(2,1)}, u32[]{:S(2)}) copy-start(bf16[2560,640]{1,0:T(8,128)(2,1)} %reshape.262) | copy-start | bytes 9830404
Sparse Core Ops, SparseCore 0:
  11.5 146.6 all-gather.14
  161.2 135.8 all-gather.16
  299.2 22.4 all-gather.10
  323.7 24.1 all-gather.12
